TPU v7x, 32 devices: a whole 2x2x4 slice. The times are simulated.
32 devices in a mesh: expert: 16 (over z, y, x), replica: 2 (over core).
Axes of the slice: x: 2, y: 2, z: 4, core: 2. Of those that a mesh axis runs over, the one named last changes fastest.
Arguments:
- tokens: bfloat16 [2048, 7168], P('expert', 'replica'), may hold values from -6 to 6
- gate_weight: bfloat16 [16, 7168, 1024], P('expert', 'replica'), may hold values from -0.0625 to 0.0625
- routes: int32 [2048, 8], P('expert'), may hold values from 0 to 15, all different within a row; in each aligned block of 128 rows (0 to 127, 128 to 255, ...) at most 80 rows name the same one
- combine: bfloat16 [2048, 8], P('expert'), may hold values from 0.099609375 to 1
- cotangent: bfloat16 [2048, 8, 1024], P('expert', None, 'replica'), may hold values from -1.5 to 1.5
Outputs:
- token_grad: bfloat16 [2048, 7168], P('expert', 'replica')
- weight_grad: bfloat16 [16, 7168, 1024], P('expert', 'replica')
Inputs may be any that keep to these rules, and one draw needn't show every extreme that they name: `routes`: each row names 8 different experts. Among the 128 rows of one index of expert (aligned blocks), no expert is named more than 80 times, and in every draw some expert is named exactly 80 times in some block.
All inputs are finite; a program needn't handle non-finite values.
Results may differ from a plain program's by a relative error of at most 0.013.
Values may be sent and summed in bfloat16 or wider, within the bound.
A program may use at most 128 MiB of HBM per device.

v0:
```python
import jax
import jax.numpy as jnp
from jax import lax
from jax.sharding import PartitionSpec as P


def silu_slope(gate):
    sig = jax.nn.sigmoid(gate)
    return sig * (1.0 + gate * (1.0 - sig))


def local(tokens, gate_weight, routes, combine, cotangent):
    n_exp = lax.axis_size("expert")
    tok_rows = tokens.shape[0]
    width = tokens.shape[1]
    topk = routes.shape[1]
    share = cotangent.shape[2]
    pairs = tok_rows * topk
    cap = max(2, pairs * 5 // (4 * n_exp))
    ids = routes.reshape(pairs)
    onehot = (ids[:, None] == jnp.arange(n_exp, dtype=jnp.int32)[None, :]).astype(jnp.int32)
    slot = jnp.sum((jnp.cumsum(onehot, axis=0) - onehot) * onehot, axis=1)
    target = ids * cap + slot
    slot_pair = (
        jnp.full((n_exp * cap,), pairs, jnp.int32)
        .at[target]
        .set(jnp.arange(pairs, dtype=jnp.int32))
    )
    x_pad = jnp.concatenate([tokens, jnp.zeros((1, width), tokens.dtype)], axis=0)
    cot_pad = jnp.concatenate(
        [cotangent.reshape(pairs, share), jnp.zeros((1, share), cotangent.dtype)], axis=0
    )
    w_pad = jnp.concatenate([combine.reshape(pairs), jnp.zeros((1,), combine.dtype)], axis=0)
    send_x = x_pad[slot_pair // topk].reshape(n_exp, cap, width)
    send_c = cot_pad[slot_pair].reshape(n_exp, cap, share)
    send_w = w_pad[slot_pair].reshape(n_exp, cap)
    recv_x, recv_c, recv_w = (
        lax.all_to_all(send_x, "expert", split_axis=0, concat_axis=0, tiled=True),
        lax.all_to_all(send_c, "expert", split_axis=0, concat_axis=0, tiled=True),
        lax.all_to_all(send_w, "expert", split_axis=0, concat_axis=0, tiled=True),
    )
    rows = n_exp * cap
    recv_x = recv_x.reshape(rows, width)
    recv_c = recv_c.reshape(rows, share)
    recv_w = recv_w.reshape(rows).astype(jnp.float32)
    weight = gate_weight[0]
    gate_part = jnp.dot(recv_x, weight, preferred_element_type=jnp.float32)
    gate_all = lax.psum(gate_part.astype(jnp.bfloat16), "replica").astype(jnp.float32)
    cot_all = lax.all_gather(recv_c, "replica", axis=1, tiled=True)
    dhid = (cot_all.astype(jnp.float32) * recv_w[:, None] * silu_slope(gate_all)).astype(
        jnp.bfloat16
    )
    back_sum = lax.dot_general(
        dhid, weight, (((1,), (1,)), ((), ())), preferred_element_type=jnp.float32
    )
    grad_sum = lax.dot_general(
        recv_x, dhid, (((0,), (0,)), ((), ())), preferred_element_type=jnp.float32
    )
    back_rows = back_sum.astype(jnp.bfloat16).reshape(n_exp, cap, width)
    arrived = lax.all_to_all(back_rows, "expert", split_axis=0, concat_axis=0, tiled=True).reshape(
        rows, width
    )
    pair_rows = arrived[target].reshape(tok_rows, topk, width)
    token_grad = jnp.sum(pair_rows.astype(jnp.float32), axis=1).astype(jnp.bfloat16)
    return (token_grad, grad_sum.astype(jnp.bfloat16)[None])


def solution(mesh):
    return jax.shard_map(
        local,
        mesh=mesh,
        in_specs=(
            P("expert", "replica"),
            P("expert", "replica", None),
            P("expert", None),
            P("expert", None),
            P("expert", None, "replica"),
        ),
        out_specs=(P("expert", "replica"), P("expert", "replica", None)),
        check_vma=False,
    )
```

profile of v0, /device:TPU:12, one launch (start us, length us, event | category | flops | bytes accessed | tf_op | source)
XLA Modules:
  0.0 581.4 jit_solution(14453779702020465772)
XLA Ops:
  7.2 0.7 broadcast_multiply_fusion
  7.9 0.8 copy.16
  8.6 0.1 eq.29
  8.7 0.1 eq.25
  8.8 0.1 copy.15
  8.9 0.1 mul.38
  9.0 4.5 reduce-window.6
  13.6 0.1 slice.16
  13.6 0.1 copy.18
  13.8 0.1 copy.19
  13.9 0.1 broadcast_add_fusion
  14.0 4.3 scatter_custom_fusion
  18.4 1.3 concatenate.9
  19.7 0.0 copy-start.1
  19.7 4.7 gather_fusion
  24.4 7.2 %all-to-all-start = ((bf16[16,80,512]{2,1,0:T(8,128)(2,1)}), bf16[16,80,512]{2,1,0:T(8,128)(2,1)S(1)}, u32[]{:S(2)}, u32[]{:S(2)}) async-start(bf16[16,80,512]{2,1,0:T(8,128)(2,1)} %bitcast.5), calls=%async_computation | async-start | bytes 2621440 | tf_op jit(solution)/shard_map/all_to_all | solution.py:39
  31.6 0.0 copy-done.1
  31.6 0.1 concatenate.11
  31.7 7.9 %gather_fusion.2 = bf16[1280,3584]{1,0:T(8,128)(2,1)} fusion(bf16[129,3584]{1,0:T(8,128)(2,1)S(1)} %concatenate.11, s32[2048]{0:T(1024)S(1)} %get-tuple-element.4), kind=kCustom, calls=%fused_computation.2 | custom fusion | bytes 18355200 | tf_op jit(solution)/shard_map/gather | solution.py:34
  39.5 23.5 %all-to-all-done = bf16[16,80,512]{2,1,0:T(8,128)(2,1)S(1)} async-done(((bf16[16,80,512]{2,1,0:T(8,128)(2,1)}), bf16[16,80,512]{2,1,0:T(8,128)(2,1)S(1)}, u32[]{:S(2)}, u32[]{:S(2)}) %all-to-all-start) | async-done | bytes 1310752 | tf_op jit(solution)/shard_map/all_to_all | solution.py:39
  63.0 0.0 copy-start
  63.0 1.1 copy-done
  64.1 4.8 all-to-all-start.2
  68.8 0.0 all-gather.2.cloned.1.call-start
  68.9 0.7 all-gather.2.cloned.1.call-update
  69.6 0.0 all-reduce.4.cloned.1.call-start
  69.6 202.2 %all-to-all-done.2 = bf16[16,80,3584]{2,1,0:T(8,128)(2,1)} async-done(((bf16[16,80,3584]{2,1,0:T(8,128)(2,1)}), bf16[16,80,3584]{2,1,0:T(8,128)(2,1)}, u32[]{:S(2)}, u32[]{:S(2)}) %all-to-all-start.2) | async-done | bytes 9175072 | tf_op jit(solution)/shard_map/all_to_all | solution.py:38
  271.8 0.0 copy-start.2
  271.8 15.3 %fusion.11 = bf16[1280,1024]{1,0:T(8,128)(2,1)} fusion(bf16[1280,3584]{1,0:T(8,128)(2,1)} %bitcast.8, bf16[1,3584,1024]{2,1,0:T(8,128)(2,1)} %param.6), kind=kOutput, calls=%fused_computation.21 | convolution fusion | flops 9396551680 | bytes 19136512 | tf_op jit(solution)/shard_map/dot_general | solution.py:47
  287.1 0.0 all-reduce.4.cloned.1.call-update
  287.1 0.0 copy-done.2
  287.1 0.1 copy.20
  287.3 0.1 reshape.94
  287.4 8.0 %gather_fusion.1 = bf16[1280]{0:T(1024)(128)(2,1)S(1)} fusion(bf16[1025]{0:T(1024)(128)(2,1)S(1)} %pad_maximum_fusion, s32[2048]{0:T(1024)S(1)} %get-tuple-element.5), kind=kCustom, calls=%fused_computation.1 | custom fusion | bytes 10240 | tf_op jit(solution)/shard_map/gather | solution.py:36
  295.4 0.1 all_to_all.20
  295.4 13.6 %all_to_all.25 = bf16[16,1,80]{2,1,0:T(2,128)(2,1)S(1)} all-to-all(bf16[16,1,80]{2,1,0:T(2,128)(2,1)S(1)} %all_to_all.20), channel_id=1, replica_groups=mesh['expert'=16,'replica'=2] {'expert'}, dimensions={0} | all-to-all | bytes 5120 | tf_op jit(solution)/shard_map/all_to_all | solution.py:40
  309.1 0.1 reshape.100
  309.2 0.0 all-gather.2.cloned.1.call-done
  309.2 3.4 all-reduce.4.cloned.1.call-done
  312.5 19.4 %convolution_convert_fusion = bf16[1280,3584]{1,0:T(8,128)(2,1)} fusion(bf16[1,3584,1024]{2,1,0:T(8,128)(2,1)} %param.6, bf16[1280,1024]{1,0:T(8,128)(2,1)} %all-reduce.4.cloned.1.call-done, bf16[1280,1024]{1,0:T(8,128)(2,1)} %all-gather.2.cloned.1.call-done, f32[1280]{0:T(1024)S(1)} %reshape.100), kind=kOutput, calls=%fused_computation.5 | convolution fusion | flops 9415557120 | bytes 21763072 | tf_op jit(solution)/shard_map/dot_general | solution.py:53
  332.0 0.0 copy-start.3
  332.0 7.2 %all-to-all-start.3 = ((bf16[16,80,3584]{2,1,0:T(8,128)(2,1)}), bf16[16,80,3584]{2,1,0:T(8,128)(2,1)}, u32[]{:S(2)}, u32[]{:S(2)}) async-start(bf16[16,80,3584]{2,1,0:T(8,128)(2,1)} %bitcast.42), calls=%async_computation.3 | async-start | bytes 18350080 | tf_op jit(solution)/shard_map/all_to_all | solution.py:60
  339.2 0.0 copy-done.3
  339.2 16.8 %fusion.3 = bf16[1,3584,1024]{2,1,0:T(8,128)(2,1)} fusion(bf16[1280,3584]{1,0:T(8,128)(2,1)} %bitcast.8, bf16[1280,1024]{1,0:T(8,128)(2,1)} %all-reduce.4.cloned.1.call-done, bf16[1280,1024]{1,0:T(8,128)(2,1)S(1)} %copy-done.3, f32[1280]{0:T(1024)S(1)} %reshape.100), kind=kOutput, calls=%fused_computation.13 | convolution fusion | flops 9414639616 | bytes 21763072 | tf_op jit(solution)/shard_map/dot_general | solution.py:56
  356.0 191.0 %all-to-all-done.3 = bf16[16,80,3584]{2,1,0:T(8,128)(2,1)} async-done(((bf16[16,80,3584]{2,1,0:T(8,128)(2,1)}), bf16[16,80,3584]{2,1,0:T(8,128)(2,1)}, u32[]{:S(2)}, u32[]{:S(2)}) %all-to-all-start.3) | async-done | bytes 9175072 | tf_op jit(solution)/shard_map/all_to_all | solution.py:60
  547.1 18.6 %gather_fusion.3 = bf16[1024,3584]{1,0:T(8,128)(2,1)} fusion(bf16[1280,3584]{1,0:T(8,128)(2,1)} %bitcast.11, s32[1024]{0:T(1024)S(1)} %broadcast_clamp_fusion), kind=kCustom, calls=%fused_computation.3 | custom fusion | bytes 14684160 | tf_op jit(solution)/shard_map/gather | solution.py:63
  565.7 8.9 %bitcast_reduce_fusion = bf16[128,3584]{1,0:T(8,128)(2,1)} fusion(bf16[1024,3584]{1,0:T(8,128)(2,1)} %gather_fusion.3), kind=kLoop, calls=%fused_computation.7 | loop fusion | flops 3211264 | bytes 8257536 | tf_op jit(solution)/shard_map/reduce_sum | solution.py:64
  (11 shorter events, 0.1 us)
Async XLA Ops:
  19.7 11.9 %copy-start.1 = (bf16[128,3584]{1,0:T(8,128)(2,1)S(1)}, bf16[128,3584]{1,0:T(8,128)(2,1)}, u32[]{:S(2)}) copy-start(bf16[128,3584]{1,0:T(8,128)(2,1)} %param.5) | copy-start | bytes 2752516
  24.4 38.6 %all-to-all-start = ((bf16[16,80,512]{2,1,0:T(8,128)(2,1)}), bf16[16,80,512]{2,1,0:T(8,128)(2,1)S(1)}, u32[]{:S(2)}, u32[]{:S(2)}) async-start(bf16[16,80,512]{2,1,0:T(8,128)(2,1)} %bitcast.5), calls=%async_computation | async-start | bytes 2621440 | tf_op jit(solution)/shard_map/all_to_all | solution.py:39
  63.0 1.1 copy-start
  64.1 207.7 %all-to-all-start.2 = ((bf16[16,80,3584]{2,1,0:T(8,128)(2,1)}), bf16[16,80,3584]{2,1,0:T(8,128)(2,1)}, u32[]{:S(2)}, u32[]{:S(2)}) async-start(bf16[16,80,3584]{2,1,0:T(8,128)(2,1)} %bitcast.41), calls=%async_computation.2 | async-start | bytes 18350080 | tf_op jit(solution)/shard_map/all_to_all | solution.py:38
  68.8 240.3 %all-gather.2.cloned.1.call-start = ((), (), s32[]{:S(2)}) async-start(), calls=%async_computation.4 | async-start | bytes 3932160 | tf_op jit(solution)/shard_map/all_gather | solution.py:49
  69.6 243.0 %all-reduce.4.cloned.1.call-start = ((), (), s32[]{:S(2)}) async-start(), calls=%async_computation.5 | async-start | bytes 5242880 | tf_op jit(solution)/shard_map/psum | solution.py:48
  271.8 15.4 %copy-start.2 = (bf16[128,8]{0,1:T(8,128)(2,1)S(1)}, bf16[128,8]{0,1:T(8,128)(2,1)}, u32[]{:S(2)}) copy-start(bf16[128,8]{0,1:T(8,128)(2,1)} %param.8) | copy-start | bytes 6148
  332.0 7.2 %copy-start.3 = (bf16[1280,1024]{1,0:T(8,128)(2,1)S(1)}, bf16[1280,1024]{1,0:T(8,128)(2,1)}, u32[]{:S(2)}) copy-start(bf16[1280,1024]{1,0:T(8,128)(2,1)} %all-gather.2.cloned.1.call-done) | copy-start | bytes 7864324
  332.0 215.1 %all-to-all-start.3 = ((bf16[16,80,3584]{2,1,0:T(8,128)(2,1)}), bf16[16,80,3584]{2,1,0:T(8,128)(2,1)}, u32[]{:S(2)}, u32[]{:S(2)}) async-start(bf16[16,80,3584]{2,1,0:T(8,128)(2,1)} %bitcast.42), calls=%async_computation.3 | async-start | bytes 18350080 | tf_op jit(solution)/shard_map/all_to_all | solution.py:60
Sparse Core Ops, SparseCore 0:
  71.2 12.4 all-gather.1
  287.2 25.2 all-reduce.3
where the time goes:
time: 583 us; the launch traced here: 581 us
  waiting for transfers between devices  421 us (72%)
  matrix products  51.6 us (9%)
  local copies, waits for them, and re-layouts  47.7 us (8%)
  starting transfers between devices  19.2 us (3%)
  other arithmetic  14.4 us (2%)
  between operations  14.2 us (2%)
  blocking collectives  13.6 us (2%)
    all_to_all x1, waiting for transfers between devices, local(): lax.all_to_all(send_x, 'expert', split_axis=0, concat_axis=0, tiled=True)  202 us
    all_to_all x1, waiting for transfers between devices, local(): lax.all_to_all(back_rows, 'expert', split_axis=0, concat_axis=0, tiled=True)  191 us
    all_to_all x1, waiting for transfers between devices, local(): lax.all_to_all(send_c, 'expert', split_axis=0, concat_axis=0, tiled=True)  23.5 us
    dot_general x1, matrix products, local(): lax.dot_general(dhid, weight, (((1,), (1,)), ((), ())), preferred_element...  19.4 us
    gather x1, local copies, waits for them, and re-layouts, local(): pair_rows = arrived[target].reshape(tok_rows, topk, width)  18.6 us
    dot_general x1, matrix products, local(): lax.dot_general(recv_x, dhid, (((0,), (0,)), ((), ())), preferred_element...  16.8 us
    dot_general x1, matrix products, local(): gate_part = jnp.dot(recv_x, weight, preferred_element_type=jnp.float32)  15.3 us
    all_to_all x1, blocking collectives, local(): lax.all_to_all(send_w, 'expert', split_axis=0, concat_axis=0, tiled=True)  13.6 us
  transfers between devices with their start and end apart: 5, of which 4 were waited for; matrix products, arithmetic and copies ran while one was open for 8% of the time, Pallas kernels for 0%

commit v1 on v0

--- a/solution.py
+++ b/solution.py
@@ -1,7 +1,11 @@
 import jax
 import jax.numpy as jnp
 from jax import lax
+from jax.experimental import pallas as pl
+from jax.experimental.pallas import tpu as pltpu
 from jax.sharding import PartitionSpec as P
+
+MESH = pl.DeviceIdType.MESH
 
 
 def silu_slope(gate):
@@ -9,7 +13,7 @@
     return sig * (1.0 + gate * (1.0 - sig))
 
 
-def local(tokens, gate_weight, routes, combine, cotangent):
+def local_routed(tokens, gate_weight, routes, combine, cotangent):
     n_exp = lax.axis_size("expert")
     tok_rows = tokens.shape[0]
     width = tokens.shape[1]
@@ -65,6 +69,341 @@
     return (token_grad, grad_sum.astype(jnp.bfloat16)[None])
 
 
+LINES = (4, 2, 2)
+ORDERS = ((0, 2, 1), (0, 1, 2), (0, 2, 1), (1, 2, 0))
+PARTS = len(ORDERS)
+STEPS = ((0, -1), (0, 1), (1, 1), (2, 1))
+
+
+def here():
+    me = lax.axis_index("expert")
+    return (me // 4, (me // 2) % 2, me % 2)
+
+
+def index_of(at):
+    return (at[0] * 2 + at[1]) * 2 + at[2]
+
+
+def moved(at, axis, by):
+    to = list(at)
+    to[axis] = at[axis] + by if axis == 0 else (at[axis] + by) % 2
+    return tuple(to)
+
+
+def inside(at):
+    return jnp.logical_and(at[0] >= 0, at[0] < LINES[0])
+
+
+def branches(order, off):
+    last = -1
+    for j, axis in enumerate(order):
+        if off[axis] != 0:
+            last = j
+    found = []
+    for way, (axis, by) in enumerate(STEPS):
+        j = order.index(axis)
+        if j > last or (j == last and axis == 0 and by * off[0] < 0):
+            found.append(way)
+    return found, (order[last] if last >= 0 else None)
+
+
+def offsets(far_first):
+    every = [
+        (dz, dy, dx)
+        for dz in range(-LINES[0] + 1, LINES[0])
+        for dy in range(2)
+        for dx in range(2)
+    ]
+    every.sort(key=lambda d: (abs(d[0]) + d[1] + d[2], abs(d[0])), reverse=far_first)
+    return every
+
+
+def greet(at):
+    barrier = pltpu.get_barrier_semaphore()
+    for axis, by in STEPS:
+        to = moved(at, axis, by)
+
+        @pl.when(inside(to))
+        def _(to=to):
+            pl.semaphore_signal(
+                barrier, inc=1, device_id={"expert": index_of(to)}, device_id_type=MESH
+            )
+
+    edge = jnp.logical_or(at[0] == 0, at[0] == LINES[0] - 1)
+
+    @pl.when(edge)
+    def _():
+        pl.semaphore_wait(barrier, 3)
+
+    @pl.when(jnp.logical_not(edge))
+    def _():
+        pl.semaphore_wait(barrier, 4)
+
+
+def spread_kernel(x_ref, all_ref, send_sem, recv_sem, own_sem):
+    at = here()
+    rows, width = x_ref.shape
+    cols = width // PARTS
+    greet(at)
+    own = pltpu.make_async_copy(
+        x_ref, all_ref.at[pl.ds(index_of(at) * rows, rows), :], own_sem
+    )
+    own.start()
+
+    def hop(part, origin, way, mine):
+        axis, by = STEPS[way]
+        span = pl.ds(part * cols, cols)
+        block = all_ref.at[pl.ds(origin * rows, rows), span]
+        return pltpu.make_async_remote_copy(
+            src_ref=x_ref.at[:, span] if mine else block,
+            dst_ref=block,
+            send_sem=send_sem.at[part * 64 + origin * 4 + way],
+            recv_sem=recv_sem.at[part * 16 + origin],
+            device_id={"expert": index_of(moved(at, axis, by))},
+            device_id_type=MESH,
+        )
+
+    def each(first):
+        for off in offsets(False):
+            mine = off == (0, 0, 0)
+            src = (at[0] + off[0], (at[1] + off[1]) % 2, (at[2] + off[2]) % 2)
+
+            @pl.when(inside(src))
+            def _(off=off, mine=mine, src=src):
+                origin = index_of(src)
+                for part, order in enumerate(ORDERS):
+                    ways, _ = branches(order, off)
+                    if first and not mine:
+                        hop(part, origin, 0, mine).wait_recv()
+                    for way in ways:
+                        axis, by = STEPS[way]
+
+                        def act(way=way):
+                            copy = hop(part, origin, way, mine)
+                            copy.start() if first else copy.wait_send()
+
+                        if axis == 0:
+                            pl.when(inside(moved(at, axis, by)))(act)
+                        else:
+                            act()
+
+    each(True)
+    each(False)
+    own.wait()
+
+
+def spread_all(tokens):
+    rows, width = tokens.shape
+    return pl.pallas_call(
+        spread_kernel,
+        out_shape=jax.ShapeDtypeStruct((16 * rows, width), tokens.dtype),
+        in_specs=[pl.BlockSpec(memory_space=pltpu.VMEM)],
+        out_specs=pl.BlockSpec(memory_space=pl.ANY),
+        scratch_shapes=[
+            pltpu.SemaphoreType.DMA((PARTS * 64,)),
+            pltpu.SemaphoreType.DMA((PARTS * 16,)),
+            pltpu.SemaphoreType.DMA,
+        ],
+        compiler_params=pltpu.CompilerParams(collective_id=0, has_side_effects=True),
+        name="spread_all",
+    )(tokens)
+
+
+def slot_plan():
+    bases, total = [], 0
+    for order in ORDERS:
+        row = []
+        for axis, by in STEPS:
+            row.append(total)
+            count = LINES[0] if axis == 0 else 1
+            for other in order[: order.index(axis)]:
+                count *= LINES[other]
+            total += count
+        bases.append(row)
+    return bases, total
+
+
+def collect_kernel(b_ref, out_ref, buf, land, send_sem, recv_sem, own_sem):
+    at = here()
+    rows, width = out_ref.shape
+    cols = width // PARTS
+    bases, _ = slot_plan()
+    own = pltpu.make_async_copy(b_ref, buf, own_sem)
+    own.start()
+    greet(at)
+    own.wait()
+
+    def slot_of(part, dest, way):
+        order = ORDERS[part]
+        axis = STEPS[way][0]
+        place = 0
+        for other in order[: order.index(axis)]:
+            place = place * LINES[other] + dest[other]
+        if axis == 0:
+            place = place * LINES[0] + dest[0]
+        return bases[part][way] + place
+
+    def pieces(act):
+        for off in offsets(True):
+            dest = (at[0] + off[0], (at[1] + off[1]) % 2, (at[2] + off[2]) % 2)
+
+            @pl.when(inside(dest))
+            def _(off=off, dest=dest):
+                for part in range(PARTS):
+                    act(part, off, dest)
+
+    def parent_copy(part, off, dest):
+        _, axis = branches(ORDERS[part], off)
+        by = 1 if axis != 0 or off[0] > 0 else -1
+        back_way = {(0, 1): 0, (0, -1): 1, (1, 1): 2, (2, 1): 3}[(axis, by)]
+        slot = slot_of(part, dest, back_way)
+        home = index_of(dest)
+        return pltpu.make_async_remote_copy(
+            src_ref=buf.at[pl.ds(home * rows, rows), pl.ds(part * cols, cols)],
+            dst_ref=land.at[slot],
+            send_sem=send_sem.at[part * 16 + home],
+            recv_sem=recv_sem.at[slot],
+            device_id={"expert": index_of(moved(at, axis, by))},
+            device_id_type=MESH,
+        )
+
+    def gather_in(part, off, dest):
+        ways, _ = branches(ORDERS[part], off)
+        home = index_of(dest)
+        span = pl.ds(part * cols, cols)
+        for way in ways:
+            axis, by = STEPS[way]
+
+            def take(way=way, axis=axis, by=by):
+                slot = slot_of(part, dest, way)
+                pltpu.make_async_remote_copy(
+                    src_ref=land.at[slot],
+                    dst_ref=land.at[slot],
+                    send_sem=recv_sem.at[slot],
+                    recv_sem=recv_sem.at[slot],
+                    device_id={"expert": index_of(moved(at, axis, by))},
+                    device_id_type=MESH,
+                ).wait_recv()
+
+                def add(i, carry):
+                    r = pl.multiple_of(i * 32, 32)
+                    line = pl.ds(pl.multiple_of(home * rows + r, 32), 32)
+                    buf[line, span] = (
+                        buf[line, span].astype(jnp.float32)
+                        + land[slot, pl.ds(r, 32), :].astype(jnp.float32)
+                    ).astype(jnp.bfloat16)
+                    return carry
+
+                lax.fori_loop(0, rows // 32, add, 0)
+
+            if axis == 0:
+                pl.when(inside(moved(at, axis, by)))(take)
+            else:
+                take()
+
+    def work(part, off, dest):
+        gather_in(part, off, dest)
+        if off != (0, 0, 0):
+            parent_copy(part, off, dest).start()
+
+    pieces(work)
+    mine = pl.ds(pl.multiple_of(index_of(at) * rows, rows), rows)
+    out_ref[...] = buf[mine, :]
+
+    def finish(part, off, dest):
+        if off != (0, 0, 0):
+            parent_copy(part, off, dest).wait_send()
+
+    pieces(finish)
+
+
+def collect(back):
+    total, width = back.shape
+    rows = total // 16
+    slots = slot_plan()[1]
+    return pl.pallas_call(
+        collect_kernel,
+        out_shape=jax.ShapeDtypeStruct((rows, width), back.dtype),
+        in_specs=[pl.BlockSpec(memory_space=pl.ANY)],
+        out_specs=pl.BlockSpec(memory_space=pltpu.VMEM),
+        scratch_shapes=[
+            pltpu.VMEM((total, width), jnp.bfloat16),
+            pltpu.VMEM((slots, rows, width // PARTS), jnp.bfloat16),
+            pltpu.SemaphoreType.DMA((PARTS * 16,)),
+            pltpu.SemaphoreType.DMA((slots,)),
+            pltpu.SemaphoreType.DMA,
+        ],
+        compiler_params=pltpu.CompilerParams(
+            collective_id=1, has_side_effects=True, vmem_limit_bytes=56 * 2**20
+        ),
+        name="collect",
+    )(back)
+
+
+def local_dense(tokens, gate_weight, routes, combine, cotangent):
+    n_exp = lax.axis_size("expert")
+    me = lax.axis_index("expert")
+    tok_rows, width = tokens.shape
+    topk = routes.shape[1]
+    hidden = gate_weight.shape[2]
+    share = cotangent.shape[2]
+    pairs = tok_rows * topk
+    cap = max(2, pairs * 5 // (4 * n_exp))
+    weight = gate_weight[0]
+    routes_all = lax.all_gather(routes, "expert", axis=0, tiled=True)
+
+    earlier = jnp.tril(jnp.ones((tok_rows, tok_rows), jnp.bfloat16), -1)
+    onehot = routes[:, :, None] == jnp.arange(n_exp, dtype=jnp.int32)[None, None, :]
+    named = jnp.any(onehot, axis=1).astype(jnp.bfloat16)
+    rank = jnp.dot(earlier, named, preferred_element_type=jnp.float32)
+    slot = jnp.sum(jnp.where(onehot, rank[:, None, :], 0.0), axis=2).astype(jnp.int32)
+    target = (routes * cap + slot).reshape(pairs)
+    pick = jnp.where(
+        jnp.arange(n_exp * cap, dtype=jnp.int32)[:, None] == target[None, :],
+        combine.reshape(pairs)[None, :],
+        jnp.zeros((), combine.dtype),
+    )
+    send_c = jnp.dot(
+        pick, cotangent.reshape(pairs, share), preferred_element_type=jnp.float32
+    ).astype(jnp.bfloat16)
+    recv_c = lax.all_to_all(
+        send_c.reshape(n_exp, cap, share), "expert", split_axis=0, concat_axis=0, tiled=True
+    )
+    recv_c = lax.all_gather(recv_c, "replica", axis=2, tiled=True)
+
+    mine = jnp.any(routes_all == me, axis=1).reshape(n_exp, tok_rows)
+    place = lax.dot_general(
+        mine.astype(jnp.bfloat16), earlier, (((1,), (1,)), ((), ())),
+        preferred_element_type=jnp.float32,
+    )
+    place = jnp.where(mine, place, -1.0).astype(jnp.int32)
+    spread = (
+        place[:, :, None] == jnp.arange(cap, dtype=jnp.int32)[None, None, :]
+    ).astype(jnp.bfloat16)
+    cot = lax.dot_general(
+        spread, recv_c, (((2,), (1,)), ((0,), (0,))), preferred_element_type=jnp.float32
+    ).astype(jnp.bfloat16).reshape(n_exp * tok_rows, hidden)
+
+    x_all = spread_all(tokens)
+    gate_part = jnp.dot(x_all, weight, preferred_element_type=jnp.float32)
+    gate_all = lax.psum(gate_part.astype(jnp.bfloat16), "replica").astype(jnp.float32)
+    dhid = (cot.astype(jnp.float32) * silu_slope(gate_all)).astype(jnp.bfloat16)
+    back = lax.dot_general(
+        dhid, weight, (((1,), (1,)), ((), ())), preferred_element_type=jnp.float32
+    ).astype(jnp.bfloat16)
+    token_grad = collect(back)
+    grad = lax.dot_general(
+        x_all, dhid, (((0,), (0,)), ((), ())), preferred_element_type=jnp.float32
+    ).astype(jnp.bfloat16)
+    return (token_grad, grad[None])
+
+
+def local(tokens, gate_weight, routes, combine, cotangent):
+    dense = lax.axis_size("expert") == 16 and tokens.shape[1] % 512 == 0
+    body = local_dense if dense else local_routed
+    return body(tokens, gate_weight, routes, combine, cotangent)
+
+
 def solution(mesh):
     return jax.shard_map(
         local,

time: 583 us -> 395 us (0.68)
  waiting for transfers between devices: 421 us -> 0.04 us
  Pallas kernels: 0 us -> 247 us
  local copies, waits for them, and re-layouts: 47.7 us -> 14.8 us
  matrix products: 51.6 us -> 71.3 us
  blocking collectives: 13.6 us -> 31.6 us
  starting transfers between devices: 19.2 us -> 7.25 us
  other arithmetic: 14.4 us -> 7.9 us
    all_to_all x3 -> x1, waiting for transfers between devices: 417 us -> 0.01 us  [local_dense(): lax.all_to_all(send_c.reshape(n_exp, cap, share), 'expert', split_axis=0,...]
    pallas_call x0 -> x2, Pallas kernels: none -> 247 us  [the longest x1 128 us: spread_all(): pl.pallas_call(spread_kernel, out_shape=jax.ShapeDtypeStruct((16 * rows,...]
    gather x4 -> x0, local copies, waits for them, and re-layouts: 39.1 us -> none  [the longest x1 18.6 us: local(): pair_rows = arrived[target].reshape(tok_rows, topk, width)]
    all_gather x0 -> x1, blocking collectives: none -> 31.6 us  [local_dense(): routes_all = lax.all_gather(routes, 'expert', axis=0, tiled=True)]
    dot_general x3 -> x7, matrix products: 51.6 us -> 71.3 us  [the longest x1 21.2 us: local_dense(): lax.dot_general(x_all, dhid, (((0,), (0,)), ((), ())), preferred_element_...]
    all_to_all x1 -> x0, blocking collectives: 13.6 us -> none  [local(): lax.all_to_all(send_w, 'expert', split_axis=0, concat_axis=0, tiled=True)]
    unnamed x10 -> x11, local copies, waits for them, and re-layouts: 1.99 us -> 14.5 us
    all_to_all x3 -> x1, starting transfers between devices: 19.1 us -> 7.17 us  [local_dense(): lax.all_to_all(send_c.reshape(n_exp, cap, share), 'expert', split_axis=0,...]
  transfers between devices with their start and end apart: 5 -> 3, of which waited for: 4 -> 0; matrix products, arithmetic and copies ran while one was open for 8% -> 7% of each run, Pallas kernels for 0% -> 32%
where the time goes in v1:
time: 395 us; the launch traced here: 394 us
  Pallas kernels  247 us (63%)
  matrix products  71.3 us (18%)
  blocking collectives  31.6 us (8%)
  local copies, waits for them, and re-layouts  14.8 us (4%)
  between operations  14.1 us (4%)
  other arithmetic  7.9 us (2%)
  starting transfers between devices  7.25 us (2%)
    pallas_call x1, Pallas kernels, spread_all(): pl.pallas_call(spread_kernel, out_shape=jax.ShapeDtypeStruct((16 * rows,...  128 us
    pallas_call x1, Pallas kernels, collect(): pl.pallas_call(collect_kernel, out_shape=jax.ShapeDtypeStruct((rows, widt...  119 us
    all_gather x1, blocking collectives, local_dense(): routes_all = lax.all_gather(routes, 'expert', axis=0, tiled=True)  31.6 us
    dot_general x1, matrix products, local_dense(): lax.dot_general(x_all, dhid, (((0,), (0,)), ((), ())), preferred_element_...  21.2 us
    dot_general x1, matrix products, local_dense(): gate_part = jnp.dot(x_all, weight, preferred_element_type=jnp.float32)  21 us
    dot_general x1, matrix products, local_dense(): lax.dot_general(dhid, weight, (((1,), (1,)), ((), ())), preferred_element...  21 us
    unnamed x11, local copies, waits for them, and re-layouts  14.5 us
  transfers between devices with their start and end apart: 3, of which 0 were waited for; matrix products, arithmetic and copies ran while one was open for 7% of the time, Pallas kernels for 32%

profile of v1, /device:TPU:12, one launch (start us, length us, event | category | flops | bytes accessed | tf_op | source)
XLA Modules:
  0.0 394.3 jit_solution(1892865374242446895)
XLA Ops:
  7.2 0.0 copy-start
  7.2 0.8 fusion.22
  8.0 0.2 fusion.24
  8.2 0.7 select_reduce_fusion
  8.9 0.7 convert_add_fusion
  9.6 0.8 copy.16
  10.4 0.1 broadcast_in_dim.51
  10.5 0.1 copy.15
  10.6 0.1 eq.56
  10.7 0.0 copy-done
  10.7 2.6 convolution_convert_fusion.2
  13.3 7.2 %all-to-all-start = ((bf16[16,80,512]{2,1,0:T(8,128)(2,1)}), bf16[16,80,512]{2,1,0:T(8,128)(2,1)S(1)}, u32[]{:S(2)}, u32[]{:S(2)}) async-start(bf16[16,80,512]{2,1,0:T(8,128)(2,1)} %bitcast.27), calls=%async_computation | async-start | bytes 2621440 | tf_op jit(solution)/shard_map/all_to_all | solution.py:369
  20.5 0.0 all-gather.2.cloned.1.call-start
  20.5 127.7 %spread_all.1 = bf16[2048,3584]{1,0:T(8,128)(2,1)} custom-call(bf16[128,3584]{1,0:T(8,128)(2,1)} %x_ref.1), custom_call_target="tpu_custom_call" | custom-call | tf_op jit(solution)/shard_map/spread_all/pallas_call | solution.py:197
  148.2 0.0 all-to-all-done
  148.3 0.0 copy-start.2
  148.3 1.1 copy-done.2
  149.3 0.0 all-gather.2.cloned.1.call-update
  149.3 0.0 copy-start.3
  149.4 0.0 all-reduce.2.cloned.1.call-start
  149.4 21.0 %fusion.12 = bf16[2048,1024]{1,0:T(8,128)(2,1)} fusion(bf16[2048,3584]{1,0:T(8,128)(2,1)} %spread_all.1, bf16[1,3584,1024]{2,1,0:T(8,128)(2,1)} %param.6), kind=kOutput, calls=%fused_computation.17 | convolution fusion | flops 15034482688 | bytes 26214400 | tf_op jit(solution)/shard_map/dot_general | solution.py:388
  170.4 0.0 all-reduce.2.cloned.1.call-update
  170.5 0.0 copy-done.3
  170.5 31.6 %all_gather.6 = s32[2048,8]{0,1:T(8,128)S(1)} all-gather(s32[128,8]{0,1:T(8,128)S(1)} %copy-done.3), channel_id=1, replica_groups=mesh['expert'=16,'replica'=2] {'expert'}, dimensions={0}, use_global_device_ids=true | all-gather | bytes 69632 | tf_op jit(solution)/shard_map/all_gather | solution.py:353
  202.2 0.2 fusion.19
  202.4 0.0 all-gather.2.cloned.1.call-done
  202.4 5.1 %convolution_convert_fusion.3 = bf16[16,128,1024]{2,1,0:T(8,128)(2,1)} fusion(bf16[16,80,1024]{2,1,0:T(8,128)(2,1)} %all-gather.2.cloned.1.call-done, s32[16,128]{1,0:T(8,128)S(1)} %fusion.19), kind=kOutput, calls=%fused_computation.19 | convolution fusion | flops 337805312 | bytes 6823936 | tf_op jit(solution)/shard_map/dot_general | solution.py:383
  207.5 0.0 all-reduce.2.cloned.1.call-done
  207.5 5.7 %fusion.6 = bf16[2048,1024]{1,0:T(8,128)(2,1)S(1)} fusion(bf16[2048,1024]{1,0:T(8,128)(2,1)} %all-reduce.2.cloned.1.call-done, bf16[16,128,1024]{2,1,0:T(8,128)(2,1)} %convolution_convert_fusion.3), kind=kLoop, calls=%fused_computation.9 | loop fusion | flops 23068672 | bytes 12582912 | tf_op jit(solution)/shard_map/convert_element_type | solution.py:390
  213.1 21.2 %fusion.10 = bf16[1,3584,1024]{1,2,0:T(8,128)(2,1)} fusion(bf16[2048,1024]{1,0:T(8,128)(2,1)S(1)} %fusion.6, bf16[2048,3584]{1,0:T(8,128)(2,1)} %spread_all.1), kind=kOutput, calls=%fused_computation.14 | convolution fusion | flops 15036055552 | bytes 26214400 | tf_op jit(solution)/shard_map/dot_general | solution.py:395
  234.3 21.0 %convolution_convert_fusion.b_ref = bf16[2048,3584]{1,0:T(8,128)(2,1)} fusion(bf16[2048,1024]{1,0:T(8,128)(2,1)S(1)} %fusion.6, bf16[1,3584,1024]{2,1,0:T(8,128)(2,1)} %param.6), kind=kOutput, calls=%fused_computation | convolution fusion | flops 15039725568 | bytes 26214400 | tf_op jit(solution)/shard_map/dot_general | solution.py:391
  255.3 0.0 copy-start.1
  255.3 10.5 %copy.17 = bf16[1,3584,1024]{2,1,0:T(8,128)(2,1)} copy(bf16[1,3584,1024]{1,2,0:T(8,128)(2,1)} %fusion.10) | data formatting | bytes 14680064
  265.8 119.5 %collect.1 = bf16[128,3584]{1,0:T(8,128)(2,1)} custom-call(bf16[2048,3584]{1,0:T(8,128)(2,1)} %convolution_convert_fusion.b_ref), custom_call_target="tpu_custom_call" | custom-call | tf_op jit(solution)/shard_map/collect/pallas_call | solution.py:324
  385.3 2.2 copy.20
  387.5 0.0 copy-done.1
  (2 shorter events, 0.0 us)
Async XLA Ops:
  7.2 3.5 copy-start
  13.3 135.0 %all-to-all-start = ((bf16[16,80,512]{2,1,0:T(8,128)(2,1)}), bf16[16,80,512]{2,1,0:T(8,128)(2,1)S(1)}, u32[]{:S(2)}, u32[]{:S(2)}) async-start(bf16[16,80,512]{2,1,0:T(8,128)(2,1)} %bitcast.27), calls=%async_computation | async-start | bytes 2621440 | tf_op jit(solution)/shard_map/all_to_all | solution.py:369
  20.5 181.9 %all-gather.2.cloned.1.call-start = ((), (), s32[]{:S(2)}) async-start(), calls=%async_computation.1 | async-start | bytes 3932160 | tf_op jit(solution)/shard_map/all_gather | solution.py:372
  148.3 1.1 copy-start.2
  149.3 21.1 %copy-start.3 = (s32[128,8]{0,1:T(8,128)S(1)}, s32[128,8]{0,1:T(8,128)}, u32[]{:S(2)}) copy-start(s32[128,8]{0,1:T(8,128)} %param.7) | copy-start | bytes 12292
  149.4 58.1 %all-reduce.2.cloned.1.call-start = ((), (), s32[]{:S(2)}) async-start(), calls=%async_computation.2 | async-start | bytes 8388608 | tf_op jit(solution)/shard_map/psum | solution.py:389
  255.3 132.1 %copy-start.1 = (bf16[128,8,512]{2,1,0:T(8,128)(2,1)S(1)}, bf16[128,8,512]{2,1,0:T(8,128)(2,1)}, u32[]{:S(2)}) copy-start(bf16[128,8,512]{2,1,0:T(8,128)(2,1)} %param.9) | copy-start | bytes 3145732
Sparse Core Ops, SparseCore 0:
  149.5 12.9 all-gather.1
  170.6 29.7 all-reduce.1

commit v2 on v1

--- a/solution.py
+++ b/solution.py
@@ -72,6 +72,7 @@
 LINES = (4, 2, 2)
 ORDERS = ((0, 2, 1), (0, 1, 2), (0, 2, 1), (1, 2, 0))
 PARTS = len(ORDERS)
+SWAPS = 4
 STEPS = ((0, -1), (0, 1), (1, 1), (2, 1))
 
 
@@ -340,66 +341,137 @@
     )(back)
 
 
+def swap_kernel(a_ref, c_ref, oa_ref, oc_ref, send_sem, recv_sem):
+    partner = {"replica": 1 - lax.axis_index("replica")}
+    barrier = pltpu.get_barrier_semaphore()
+    pl.semaphore_signal(barrier, inc=1, device_id=partner, device_id_type=MESH)
+    pl.semaphore_wait(barrier, 1)
+    copies = []
+    for src, dst in ((c_ref, oc_ref), (a_ref, oa_ref)):
+        rows = src.shape[0] // SWAPS
+        for i in range(SWAPS):
+            n = len(copies)
+            copies.append(
+                pltpu.make_async_remote_copy(
+                    src_ref=src.at[pl.ds(i * rows, rows), :],
+                    dst_ref=dst.at[pl.ds(i * rows, rows), :],
+                    send_sem=send_sem.at[n],
+                    recv_sem=recv_sem.at[n],
+                    device_id=partner,
+                    device_id_type=MESH,
+                )
+            )
+    for copy in copies:
+        copy.start()
+    for copy in copies:
+        copy.wait()
+
+
+def swap(a, c):
+    return pl.pallas_call(
+        swap_kernel,
+        out_shape=(
+            jax.ShapeDtypeStruct(a.shape, a.dtype),
+            jax.ShapeDtypeStruct(c.shape, c.dtype),
+        ),
+        in_specs=[pl.BlockSpec(memory_space=pl.ANY)] * 2,
+        out_specs=[pl.BlockSpec(memory_space=pl.ANY)] * 2,
+        scratch_shapes=[
+            pltpu.SemaphoreType.DMA((2 * SWAPS,)),
+            pltpu.SemaphoreType.DMA((2 * SWAPS,)),
+        ],
+        compiler_params=pltpu.CompilerParams(collective_id=2, has_side_effects=True),
+        name="swap",
+    )(a, c)
+
+
+def weight_sum_kernel(x_ref, d_ref, o_ref):
+    o_ref[...] = lax.dot_general(
+        x_ref[...], d_ref[...], (((0,), (0,)), ((), ())), preferred_element_type=jnp.float32
+    ).astype(o_ref.dtype)
+
+
+def weight_sum(x_all, dhid):
+    total, width = x_all.shape
+    hidden = dhid.shape[1]
+    return pl.pallas_call(
+        weight_sum_kernel,
+        out_shape=jax.ShapeDtypeStruct((width, hidden), jnp.bfloat16),
+        grid=(width // 512,),
+        in_specs=[
+            pl.BlockSpec((total, 512), lambda i: (0, i)),
+            pl.BlockSpec((total, hidden), lambda i: (0, 0)),
+        ],
+        out_specs=pl.BlockSpec((512, hidden), lambda i: (i, 0)),
+        compiler_params=pltpu.CompilerParams(vmem_limit_bytes=48 * 2**20),
+        name="weight_sum",
+    )(x_all, dhid)
+
+
 def local_dense(tokens, gate_weight, routes, combine, cotangent):
     n_exp = lax.axis_size("expert")
-    me = lax.axis_index("expert")
     tok_rows, width = tokens.shape
     topk = routes.shape[1]
-    hidden = gate_weight.shape[2]
     share = cotangent.shape[2]
     pairs = tok_rows * topk
     cap = max(2, pairs * 5 // (4 * n_exp))
     weight = gate_weight[0]
-    routes_all = lax.all_gather(routes, "expert", axis=0, tiled=True)
-
     earlier = jnp.tril(jnp.ones((tok_rows, tok_rows), jnp.bfloat16), -1)
     onehot = routes[:, :, None] == jnp.arange(n_exp, dtype=jnp.int32)[None, None, :]
     named = jnp.any(onehot, axis=1).astype(jnp.bfloat16)
     rank = jnp.dot(earlier, named, preferred_element_type=jnp.float32)
     slot = jnp.sum(jnp.where(onehot, rank[:, None, :], 0.0), axis=2).astype(jnp.int32)
     target = (routes * cap + slot).reshape(pairs)
-    pick = jnp.where(
-        jnp.arange(n_exp * cap, dtype=jnp.int32)[:, None] == target[None, :],
-        combine.reshape(pairs)[None, :],
-        jnp.zeros((), combine.dtype),
-    )
+    taken = jnp.arange(n_exp * cap, dtype=jnp.int32)[:, None] == target[None, :]
+    pick = jnp.where(taken, combine.reshape(pairs)[None, :], jnp.zeros((), combine.dtype))
     send_c = jnp.dot(
         pick, cotangent.reshape(pairs, share), preferred_element_type=jnp.float32
     ).astype(jnp.bfloat16)
-    recv_c = lax.all_to_all(
-        send_c.reshape(n_exp, cap, share), "expert", split_axis=0, concat_axis=0, tiled=True
-    )
-    recv_c = lax.all_gather(recv_c, "replica", axis=2, tiled=True)
-
-    mine = jnp.any(routes_all == me, axis=1).reshape(n_exp, tok_rows)
-    place = lax.dot_general(
-        mine.astype(jnp.bfloat16), earlier, (((1,), (1,)), ((), ())),
-        preferred_element_type=jnp.float32,
-    )
-    place = jnp.where(mine, place, -1.0).astype(jnp.int32)
+    token_of = jnp.broadcast_to(
+        (jnp.arange(pairs, dtype=jnp.int32) // topk)[:, None], (pairs, 128)
+    ).astype(jnp.bfloat16)
+    send_t = jnp.dot(
+        taken.astype(jnp.bfloat16), token_of, preferred_element_type=jnp.float32
+    ).astype(jnp.bfloat16)
+    recv = lax.all_to_all(
+        jnp.concatenate([send_c, send_t], axis=1).reshape(n_exp, cap, share + 128),
+        "expert", split_axis=0, concat_axis=0, tiled=True,
+    )
+
+    x_all = spread_all(tokens)
+    gate_part = jnp.dot(x_all, weight, preferred_element_type=jnp.float32)
+    gate_part = gate_part.astype(jnp.bfloat16)
     spread = (
-        place[:, :, None] == jnp.arange(cap, dtype=jnp.int32)[None, None, :]
+        recv[:, :, share].astype(jnp.int32)[:, None, :]
+        == jnp.arange(tok_rows, dtype=jnp.int32)[None, :, None]
     ).astype(jnp.bfloat16)
     cot = lax.dot_general(
-        spread, recv_c, (((2,), (1,)), ((0,), (0,))), preferred_element_type=jnp.float32
-    ).astype(jnp.bfloat16).reshape(n_exp * tok_rows, hidden)
-
-    x_all = spread_all(tokens)
-    gate_part = jnp.dot(x_all, weight, preferred_element_type=jnp.float32)
-    gate_all = lax.psum(gate_part.astype(jnp.bfloat16), "replica").astype(jnp.float32)
+        spread, recv[:, :, :share], (((2,), (1,)), ((0,), (0,))),
+        preferred_element_type=jnp.float32,
+    ).astype(jnp.bfloat16).reshape(n_exp * tok_rows, share)
+    gate_other, cot_other = swap(gate_part, cot)
+    gate_all = gate_part.astype(jnp.float32) + gate_other.astype(jnp.float32)
+    cot = jnp.where(
+        lax.axis_index("replica") == 0,
+        jnp.concatenate([cot, cot_other], axis=1),
+        jnp.concatenate([cot_other, cot], axis=1),
+    )
     dhid = (cot.astype(jnp.float32) * silu_slope(gate_all)).astype(jnp.bfloat16)
     back = lax.dot_general(
         dhid, weight, (((1,), (1,)), ((), ())), preferred_element_type=jnp.float32
     ).astype(jnp.bfloat16)
     token_grad = collect(back)
-    grad = lax.dot_general(
-        x_all, dhid, (((0,), (0,)), ((), ())), preferred_element_type=jnp.float32
-    ).astype(jnp.bfloat16)
+    grad = weight_sum(x_all, dhid)
     return (token_grad, grad[None])
 
 
 def local(tokens, gate_weight, routes, combine, cotangent):
-    dense = lax.axis_size("expert") == 16 and tokens.shape[1] % 512 == 0
+    dense = (
+        lax.axis_size("expert") == 16
+        and lax.axis_size("replica") == 2
+        and tokens.shape[0] == 128
+        and tokens.shape[1] % 512 == 0
+    )
     body = local_dense if dense else local_routed
     return body(tokens, gate_weight, routes, combine, cotangent)
 

time: 395 us -> 359 us (0.909)
  Pallas kernels: 247 us -> 285 us
  blocking collectives: 31.6 us -> 0 us
  matrix products: 71.3 us -> 47.6 us
  between operations: 14.1 us -> 0.74 us
  local copies, waits for them, and re-layouts: 14.8 us -> 5.49 us
  other arithmetic: 7.9 us -> 12.5 us
    all_gather x1 -> x0, blocking collectives: 31.6 us -> none  [local_dense(): routes_all = lax.all_gather(routes, 'expert', axis=0, tiled=True)]
    pallas_call x0 -> x2, Pallas kernels: none -> 29.8 us  [the longest x1 19.2 us: weight_sum(): pl.pallas_call(weight_sum_kernel, out_shape=jax.ShapeDtypeStruct((width,...]
    dot_general x3 -> x2, matrix products: 26.5 us -> 3.83 us  [the longest x1 2.7 us: local_dense(): lax.dot_general(spread, recv[:, :, :share], (((2,), (1,)), ((0,), (0,))),...]
    unnamed x11 -> x6, local copies, waits for them, and re-layouts: 14.5 us -> 2.97 us
    pallas_call x1, Pallas kernels: 128 us -> 133 us  [spread_all(): pl.pallas_call(spread_kernel, out_shape=jax.ShapeDtypeStruct((16 * rows,...]
    convert_element_type x1, other arithmetic: 5.65 us -> 9.82 us  [local_dense(): dhid = (cot.astype(jnp.float32) * silu_slope(gate_all)).astype(jnp.bfloat16)]
  transfers between devices with their start and end apart: 3 -> 1, of which waited for: 0 -> 0; matrix products, arithmetic and copies ran while one was open for 7% -> 6% of each run, Pallas kernels for 32% -> 37%
where the time goes in v2:
time: 359 us
  Pallas kernels  285 us (79%)
  matrix products  47.6 us (13%)
  other arithmetic  12.5 us (3%)
  starting transfers between devices  7.17 us (2%)
  local copies, waits for them, and re-layouts  5.49 us (2%)
    pallas_call x1, Pallas kernels, spread_all(): pl.pallas_call(spread_kernel, out_shape=jax.ShapeDtypeStruct((16 * rows,...  133 us
    pallas_call x1, Pallas kernels, collect(): pl.pallas_call(collect_kernel, out_shape=jax.ShapeDtypeStruct((rows, widt...  122 us
    dot_general x1, matrix products, local_dense(): gate_part = jnp.dot(x_all, weight, preferred_element_type=jnp.float32)  21 us
    dot_general x1, matrix products, local_dense(): lax.dot_general(dhid, weight, (((1,), (1,)), ((), ())), preferred_element...  21 us
    pallas_call x1, Pallas kernels, weight_sum(): pl.pallas_call(weight_sum_kernel, out_shape=jax.ShapeDtypeStruct((width,...  19.2 us
    pallas_call x1, Pallas kernels, swap(): pl.pallas_call(swap_kernel, out_shape=(jax.ShapeDtypeStruct(a.shape, a.dt...  10.6 us
    convert_element_type x1, other arithmetic, local_dense(): dhid = (cot.astype(jnp.float32) * silu_slope(gate_all)).astype(jnp.bfloat16)  9.82 us
  transfers between devices with their start and end apart: 1, of which 0 were waited for; matrix products, arithmetic and copies ran while one was open for 6% of the time, Pallas kernels for 37%

profile of v2, /device:TPU:12, one launch (start us, length us, event | category | flops | bytes accessed | tf_op | source)
XLA Modules:
  0.0 359.0 jit_solution(1326041965719453049)
XLA Ops:
  0.6 0.0 copy-start
  0.7 0.8 fusion.18
  1.5 0.2 fusion.20
  1.7 0.7 select_reduce_fusion
  2.4 0.7 convert_add_fusion
  3.1 0.8 copy.16
  3.9 0.1 broadcast_in_dim.52
  4.0 0.1 copy.15
  4.1 0.1 eq.49
  4.2 1.1 fusion.11
  5.3 0.0 copy-done
  5.3 1.6 convolution_convert_fusion.1
  6.9 0.1 pad_maximum_fusion
  7.0 2.2 copy.17
  9.2 7.2 %all-to-all-start = ((bf16[16,80,640]{2,1,0:T(8,128)(2,1)}), bf16[16,80,640]{2,1,0:T(8,128)(2,1)S(1)}, u32[]{:S(2)}, u32[]{:S(2)}) async-start(bf16[16,80,640]{2,1,0:T(8,128)(2,1)} %bitcast.19), calls=%async_computation | async-start | bytes 3276800 | tf_op jit(solution)/shard_map/all_to_all | solution.py:436
  16.4 133.5 %spread_all.1.x_ref = bf16[2048,3584]{1,0:T(8,128)(2,1)} custom-call(bf16[128,3584]{1,0:T(8,128)(2,1)} %x_ref.1), custom_call_target="tpu_custom_call" | custom-call | tf_op jit(solution)/shard_map/spread_all/pallas_call | solution.py:198
  149.9 21.0 %fusion.5.a_ref = bf16[2048,1024]{1,0:T(8,128)(2,1)} fusion(bf16[2048,3584]{1,0:T(8,128)(2,1)} %spread_all.1.x_ref, bf16[1,3584,1024]{2,1,0:T(8,128)(2,1)} %param.6), kind=kOutput, calls=%fused_computation.9 | convolution fusion | flops 15034482688 | bytes 26214400 | tf_op jit(solution)/shard_map/dot_general | solution.py:442
  170.9 0.0 all-to-all-done
  170.9 0.3 convert_reduce_fusion
  171.3 2.7 convolution_convert_fusion.2
  174.0 10.6 %swap.1 = (bf16[2048,1024]{1,0:T(8,128)(2,1)}, bf16[2048,512]{1,0:T(8,128)(2,1)}) custom-call(bf16[2048,1024]{1,0:T(8,128)(2,1)} %fusion.5.a_ref, bf16[2048,512]{1,0:T(8,128)(2,1)} %bitcast.16), custom_call_target="tpu_custom_call" | custom-call | tf_op jit(solution)/shard_map/swap/pallas_call | solution.py:371
  184.6 9.8 %multiply_convert_fusion.d_ref = bf16[2048,1024]{1,0:T(8,128)(2,1)S(1)} fusion(bf16[2048,1024]{1,0:T(8,128)(2,1)} %get-tuple-element.5, bf16[2048,1024]{1,0:T(8,128)(2,1)} %fusion.5.a_ref, bf16[2048,512]{1,0:T(8,128)(2,1)} %get-tuple-element.4, bf16[2048,512]{1,0:T(8,128)(2,1)} %bitcast.17, pred[]{:T(512)S(6)} %eq.44), kind=kLoop, calls=%fused_computation.1 | loop fusion | flops 46137344 | bytes 16777216 | tf_op jit(solution)/shard_map/convert_element_type | solution.py:459
  194.4 19.2 %weight_sum.1 = bf16[3584,1024]{1,0:T(8,128)(2,1)} custom-call(bf16[2048,3584]{1,0:T(8,128)(2,1)} %spread_all.1.x_ref, bf16[2048,1024]{1,0:T(8,128)(2,1)S(1)} %multiply_convert_fusion.d_ref), custom_call_target="tpu_custom_call" | custom-call | tf_op jit(solution)/shard_map/weight_sum/pallas_call | solution.py:397
  213.6 21.0 %convolution_convert_fusion.b_ref = bf16[2048,3584]{1,0:T(8,128)(2,1)} fusion(bf16[2048,1024]{1,0:T(8,128)(2,1)S(1)} %multiply_convert_fusion.d_ref, bf16[1,3584,1024]{2,1,0:T(8,128)(2,1)} %param.6), kind=kOutput, calls=%fused_computation | convolution fusion | flops 15039725568 | bytes 26214400 | tf_op jit(solution)/shard_map/dot_general | solution.py:460
  234.6 0.0 copy-start.1
  234.6 122.2 %collect.1 = bf16[128,3584]{1,0:T(8,128)(2,1)} custom-call(bf16[2048,3584]{1,0:T(8,128)(2,1)} %convolution_convert_fusion.b_ref), custom_call_target="tpu_custom_call" | custom-call | tf_op jit(solution)/shard_map/collect/pallas_call | solution.py:325
  356.8 2.2 copy.19
  359.0 0.0 copy-done.1
  (2 shorter events, 0.0 us)
Async XLA Ops:
  0.6 4.7 %copy-start = (bf16[128,8,512]{2,1,0:T(8,128)(2,1)S(1)}, bf16[128,8,512]{2,1,0:T(8,128)(2,1)}, u32[]{:S(2)}) copy-start(bf16[128,8,512]{2,1,0:T(8,128)(2,1)} %param.9) | copy-start | bytes 3145732
  9.2 161.7 %all-to-all-start = ((bf16[16,80,640]{2,1,0:T(8,128)(2,1)}), bf16[16,80,640]{2,1,0:T(8,128)(2,1)S(1)}, u32[]{:S(2)}, u32[]{:S(2)}) async-start(bf16[16,80,640]{2,1,0:T(8,128)(2,1)} %bitcast.19), calls=%async_computation | async-start | bytes 3276800 | tf_op jit(solution)/shard_map/all_to_all | solution.py:436
  234.6 124.3 %copy-start.1 = (bf16[128,8,512]{2,1,0:T(8,128)(2,1)S(1)}, bf16[128,8,512]{2,1,0:T(8,128)(2,1)}, u32[]{:S(2)}) copy-start(bf16[128,8,512]{2,1,0:T(8,128)(2,1)} %param.9) | copy-start | bytes 3145732
